TPU v7x, 32 devices: a whole 2x2x4 slice. The times are simulated.
32 devices in a mesh: fsdp: 8 (over z, x), mat: 4 (over y, core).
Axes of the slice: x: 2, y: 2, z: 4, core: 2. Of those that a mesh axis runs over, the one named last changes fastest.
Arguments:
- grads: bfloat16 [4, 8192, 16384], P('mat', 'fsdp'), may hold values from -5000 to 5000
- p_old: bfloat16 [4, 8192, 256], P('mat', 'fsdp'), may hold values from -2 to 2
- p_new: bfloat16 [4, 8192, 256], P('mat', 'fsdp'), may hold values from -2 to 2
- m_old: float32 [4, 16384, 256], P('mat', 'fsdp'), may hold values from -4 to 4
- v_old: float32 [4, 16384, 256], P('mat', 'fsdp'), may hold values from 0.003 to 0.03
Outputs:
- update: bfloat16 [4, 8192, 16384], P('mat', 'fsdp')
- m_new: float32 [4, 16384, 256], P('mat', 'fsdp')
- v_new: float32 [4, 16384, 256], P('mat', 'fsdp')
All inputs are finite; a program needn't handle non-finite values.
Results may differ from a plain program's by a relative error of at most 0.0046.
Values may be sent and summed in bfloat16 or wider, within the bound.
A program may use at most 320 MiB of HBM per device.

v0:
```python
import jax
import jax.numpy as jnp
from jax import lax
from jax.sharding import PartitionSpec as P

D = 8192
COLS = 16384


def shards(grads, p_old, p_new, m_old, v_old):
    grad = grads[0]
    basis_old = p_old[0]
    basis_new = p_new[0]
    first_old = m_old[0]
    second_old = v_old[0]
    total = lax.psum(jnp.sum(jnp.square(grad.astype(jnp.float32))), ("fsdp", "mat"))
    mat_count = lax.axis_size("mat")
    clip = jnp.minimum(1.0, 0.5 / jnp.sqrt(total / (mat_count * D * COLS) + 1e-06))
    partial_gram = lax.dot_general(
        basis_new, basis_old, (((0,), (0,)), ((), ())), preferred_element_type=jnp.float32
    )
    gram = lax.psum(partial_gram, "fsdp")
    rot_m = jnp.dot(first_old, gram.T, precision=lax.Precision.HIGHEST)
    rot_v = jnp.dot(second_old, (gram * gram).T, precision=lax.Precision.HIGHEST)
    proj = clip * lax.psum_scatter(
        lax.dot_general(
            grad, basis_new, (((0,), (0,)), ((), ())), preferred_element_type=jnp.float32
        ),
        "fsdp",
        scatter_dimension=0,
        tiled=True,
    )
    first = 0.9 * rot_m + 0.1 * proj
    second = 0.99 * rot_v + 0.01 * proj * proj
    dirn = (first / (jnp.sqrt(second) + 1e-08)).astype(jnp.bfloat16)
    upd = lax.dot_general(
        basis_new,
        lax.all_gather(dirn, "fsdp", axis=0, tiled=True),
        (((1,), (1,)), ((), ())),
        preferred_element_type=jnp.float32,
    ).astype(jnp.bfloat16)
    return (upd[None], first[None], second[None])


def solution(mesh):
    placed = (
        P("mat", "fsdp", None),
        P("mat", "fsdp", None),
        P("mat", "fsdp", None),
        P("mat", "fsdp", None),
        P("mat", "fsdp", None),
    )
    return jax.shard_map(
        shards,
        mesh=mesh,
        in_specs=placed,
        out_specs=(P("mat", "fsdp", None), P("mat", "fsdp", None), P("mat", "fsdp", None)),
        check_vma=False,
    )
```

profile of v0, /device:TPU:0, one launch (start us, length us, event | category | flops | bytes accessed | tf_op | source)
XLA Modules:
  0.0 569.8 jit_solution(3575329393713956755)
XLA Ops:
  7.2 0.0 copy-start
  7.2 0.0 all-reduce.2.cloned.1.call-start
  7.2 2.4 fusion.8
  9.6 0.0 all-reduce.2.cloned.1.call-update
  9.6 0.0 reduce-scatter.2.cloned.1.call-start
  9.7 18.8 %fusion = f32[16384,256]{0,1:T(8,128)} fusion(bf16[1,1024,16384]{2,1,0:T(8,128)(2,1)} %param.5, bf16[1,1024,256]{2,1,0:T(8,128)(2,1)} %param.7), kind=kOutput, calls=%fused_computation.1 | convolution fusion | flops 8589934592 | bytes 50855936 | tf_op jit(solution)/shard_map/dot_general | solution.py:26
  28.5 0.0 reduce-scatter.2.cloned.1.call-update
  28.6 0.0 all-gather.2.cloned.1.call-start
  28.6 19.6 %multiply_reduce_fusion = f32[]{:T(128)} fusion(bf16[1,1024,16384]{2,1,0:T(8,128)(2,1)} %param.5), kind=kLoop, calls=%fused_computation | loop fusion | flops 50331648 | bytes 33554436 | tf_op jit(solution)/shard_map/reduce_sum | solution.py:16
  48.2 42.4 %psum.15 = f32[]{:T(128)} all-reduce(f32[]{:T(128)} %multiply_reduce_fusion), channel_id=1, replica_groups=mesh['fsdp'=8,'mat'=4] {'fsdp','mat'}, use_global_device_ids=true, to_apply=%region_2.0 | all-reduce | flops 1 | bytes 8 | tf_op jit(solution)/shard_map/psum | solution.py:16
  91.3 0.0 all-reduce.2.cloned.1.call-done
  91.3 0.0 copy-start.6
  91.3 277.4 %reduce-scatter.2.cloned.1.call-done = f32[2048,256]{0,1:T(8,128)} async-done(((f32[16384,256]{0,1:T(8,128)}), f32[2048,256]{0,1:T(8,128)}) %reduce-scatter.2.cloned.1.call-update) | async-done | bytes 2097168 | tf_op jit(solution)/shard_map/reduce_scatter | solution.py:25
  368.8 0.0 copy-start.5
  368.8 4.6 fusion.3
  373.4 0.0 copy-done
  373.4 0.0 copy-done.6
  373.4 0.0 copy-done.5
  373.4 0.0 copy-start.2
  373.4 4.5 divide_convert_fusion
  377.9 0.0 copy-done.2
  377.9 0.0 all-gather.2.cloned.1.call-update
  378.0 0.0 copy-start.3
  378.0 3.0 copy.10
  381.0 0.0 copy-done.3
  381.0 0.0 copy-start.4
  381.0 1.8 copy.11
  382.8 118.8 %all-gather.2.cloned.1.call-done = bf16[16384,256]{0,1:T(8,128)(2,1)} async-done(((bf16[2048,256]{0,1:T(8,128)(2,1)}), bf16[16384,256]{0,1:T(8,128)(2,1)}) %all-gather.2.cloned.1.call-update) | async-done | bytes 8388624 | tf_op jit(solution)/shard_map/all_gather | solution.py:38
  501.7 0.0 copy-done.4
  501.7 17.5 %convert_bitcast_fusion = bf16[1,1024,16384]{1,2,0:T(8,128)(2,1)} fusion(bf16[16384,256]{0,1:T(8,128)(2,1)} %all-gather.2.cloned.1.call-done, bf16[1,1024,256]{2,1,0:T(8,128)(2,1)S(1)} %copy-done.4), kind=kOutput, calls=%fused_computation.3 | convolution fusion | flops 8606711808 | bytes 42467328 | tf_op jit(solution)/shard_map/dot_general | solution.py:36
  519.2 44.0 %copy.9 = bf16[1,1024,16384]{2,1,0:T(8,128)(2,1)} copy(bf16[1,1024,16384]{1,2,0:T(8,128)(2,1)} %convert_bitcast_fusion) | data formatting | bytes 67108864
  563.2 0.0 copy-done.1
  (1 shorter events, 0.0 us)
Async XLA Ops:
  7.2 366.2 %copy-start = (f32[1,2048,256]{2,1,0:T(8,128)S(1)}, f32[1,2048,256]{2,1,0:T(8,128)}, u32[]{:S(2)}) copy-start(f32[1,2048,256]{2,1,0:T(8,128)} %param.8) | copy-start | bytes 6291460
  7.2 84.1 %all-reduce.2.cloned.1.call-start = ((), (), s32[]{:S(2)}) async-start(), calls=%async_computation.1 | async-start | bytes 524288 | tf_op jit(solution)/shard_map/psum | solution.py:22
  9.6 359.1 %reduce-scatter.2.cloned.1.call-start = ((), (), s32[]{:S(2)}) async-start(), calls=%async_computation.2 | async-start | bytes 18874368 | tf_op jit(solution)/shard_map/reduce_scatter | solution.py:25
  28.6 473.1 %all-gather.2.cloned.1.call-start = ((), (), s32[]{:S(2)}) async-start(), calls=%async_computation.3 | async-start | bytes 9437184 | tf_op jit(solution)/shard_map/all_gather | solution.py:38
  91.3 282.1 %copy-start.6 = (f32[256,256]{1,0:T(8,128)S(1)}, f32[256,256]{1,0:T(8,128)}, u32[]{:S(2)}) copy-start(f32[256,256]{1,0:T(8,128)} %all-reduce.2.cloned.1.call-done) | copy-start | bytes 786436
  368.8 4.7 copy-start.5
  373.4 4.5 copy-start.2
  378.0 3.0 copy-start.3
  381.0 120.7 %copy-start.4 = (bf16[1,1024,256]{2,1,0:T(8,128)(2,1)S(1)}, bf16[1,1024,256]{2,1,0:T(8,128)(2,1)}, u32[]{:S(2)}) copy-start(bf16[1,1024,256]{2,1,0:T(8,128)(2,1)} %param.7) | copy-start | bytes 1572868
  519.2 44.0 %copy-start.1 = (f32[1,2048,256]{2,1,0:T(8,128)S(1)}, f32[1,2048,256]{2,1,0:T(8,128)}, u32[]{:S(2)}) copy-start(f32[1,2048,256]{2,1,0:T(8,128)} %param.8) | copy-start | bytes 6291460
Sparse Core Ops, SparseCore 0:
  11.9 73.7 all-reduce.1
  90.1 278.6 reduce-scatter.1
  378.1 123.5 all-gather.1
where the time goes:
time: 571 us; the launch traced here: 570 us
  waiting for transfers between devices  396 us (69%)
  local copies, waits for them, and re-layouts  48.9 us (9%)
  matrix products  47.9 us (8%)
  blocking collectives  42.4 us (7%)
  other arithmetic  19.6 us (3%)
  between operations  14.5 us (3%)
    reduce_scatter x1, waiting for transfers between devices, shards(): lax.psum_scatter(lax.dot_general(grad, basis_new, (((0,), (0,)), ((), ())...  277 us
    all_gather x1, waiting for transfers between devices, shards(): lax.all_gather(dirn, 'fsdp', axis=0, tiled=True)  119 us
    unnamed x17, local copies, waits for them, and re-layouts  48.9 us
    psum x1, blocking collectives, shards(): lax.psum(jnp.sum(jnp.square(grad.astype(jnp.float32))), ('fsdp', 'mat'))  42.4 us
    reduce_sum x1, other arithmetic, shards(): jnp.sum(jnp.square(grad.astype(jnp.float32)))  19.6 us
    dot_general x1, matrix products, shards(): lax.dot_general(grad, basis_new, (((0,), (0,)), ((), ())), preferred_elem...  18.8 us
    dot_general x1, matrix products, shards(): lax.dot_general(basis_new, lax.all_gather(dirn, 'fsdp', axis=0, tiled=Tru...  17.5 us
  transfers between devices with their start and end apart: 3, of which 2 were waited for; matrix products, arithmetic and copies ran while one was open for 8% of the time, Pallas kernels for 0%

commit v1 on v0

--- a/solution.py
+++ b/solution.py
@@ -5,6 +5,18 @@
 
 D = 8192
 COLS = 16384
+
+
+def collect(x, axis, dim):
+    ways, here = (lax.axis_size(axis), lax.axis_index(axis))
+    grown, reach = (x, 1)
+    while reach < ways:
+        theirs = lax.ppermute(grown, axis, [(d, d ^ reach) for d in range(ways)])
+        mine_first = jnp.concatenate([grown, theirs], axis=dim)
+        theirs_first = jnp.concatenate([theirs, grown], axis=dim)
+        grown = jnp.where(here & reach == 0, mine_first, theirs_first)
+        reach = 2 * reach
+    return grown
 
 
 def shards(grads, p_old, p_new, m_old, v_old):
@@ -35,7 +47,7 @@
     dirn = (first / (jnp.sqrt(second) + 1e-08)).astype(jnp.bfloat16)
     upd = lax.dot_general(
         basis_new,
-        lax.all_gather(dirn, "fsdp", axis=0, tiled=True),
+        collect(dirn, "fsdp", 0),
         (((1,), (1,)), ((), ())),
         preferred_element_type=jnp.float32,
     ).astype(jnp.bfloat16)

time: 571 us -> 713 us (1.25)
  waiting for transfers between devices: 396 us -> 521 us
    ppermute x0 -> x3, waiting for transfers between devices: none -> 243 us  [collect(): theirs = lax.ppermute(grown, axis, [(d, d ^ reach) for d in range(ways)])]
    all_gather x1 -> x0, waiting for transfers between devices: 119 us -> none  [shards(): lax.all_gather(dirn, 'fsdp', axis=0, tiled=True)]
  transfers between devices with their start and end apart: 3 -> 5, of which waited for: 2 -> 4; matrix products, arithmetic and copies ran while one was open for 8% -> 6% of each run, Pallas kernels for 0% -> 0%
where the time goes in v1:
time: 713 us; the launch traced here: 711 us
  waiting for transfers between devices  521 us (73%)
  matrix products  53.1 us (7%)
  local copies, waits for them, and re-layouts  48.8 us (7%)
  blocking collectives  42.5 us (6%)
  other arithmetic  26.6 us (4%)
  between operations  14.8 us (2%)
    reduce_scatter x1, waiting for transfers between devices, shards(): lax.psum_scatter(lax.dot_general(grad, basis_new, (((0,), (0,)), ((), ())...  278 us
    ppermute x3, waiting for transfers between devices, collect(): theirs = lax.ppermute(grown, axis, [(d, d ^ reach) for d in range(ways)])  243 us
    unnamed x17, local copies, waits for them, and re-layouts  48.8 us
    psum x1, blocking collectives, shards(): lax.psum(jnp.sum(jnp.square(grad.astype(jnp.float32))), ('fsdp', 'mat'))  42.5 us
    dot_general x1, matrix products, shards(): lax.dot_general(basis_new, collect(dirn, 'fsdp', 0), (((1,), (1,)), ((),...  23.1 us
    reduce_sum x1, other arithmetic, shards(): jnp.sum(jnp.square(grad.astype(jnp.float32)))  19.6 us
    dot_general x1, matrix products, shards(): lax.dot_general(grad, basis_new, (((0,), (0,)), ((), ())), preferred_elem...  18.8 us
  transfers between devices with their start and end apart: 5, of which 4 were waited for; matrix products, arithmetic and copies ran while one was open for 6% of the time, Pallas kernels for 0%

profile of v1, /device:TPU:0, one launch (start us, length us, event | category | flops | bytes accessed | tf_op | source)
XLA Modules:
  0.0 711.2 jit_solution(4851754070093124563)
XLA Ops:
  7.2 0.0 copy-start
  7.2 0.0 all-reduce.2.cloned.1.call-start
  7.2 2.4 fusion.14
  9.6 0.0 all-reduce.2.cloned.1.call-update
  9.6 0.0 reduce-scatter.2.cloned.1.call-start
  9.7 18.8 %fusion = f32[16384,256]{0,1:T(8,128)} fusion(bf16[1,1024,16384]{2,1,0:T(8,128)(2,1)} %param.5, bf16[1,1024,256]{2,1,0:T(8,128)(2,1)} %param.7), kind=kOutput, calls=%fused_computation.1 | convolution fusion | flops 8589934592 | bytes 50855936 | tf_op jit(solution)/shard_map/dot_general | solution.py:38
  28.5 0.0 reduce-scatter.2.cloned.1.call-update
  28.6 19.6 %multiply_reduce_fusion = f32[]{:T(128)} fusion(bf16[1,1024,16384]{2,1,0:T(8,128)(2,1)} %param.5), kind=kLoop, calls=%fused_computation | loop fusion | flops 50331648 | bytes 33554436 | tf_op jit(solution)/shard_map/reduce_sum | solution.py:28
  48.1 42.5 %psum.15 = f32[]{:T(128)} all-reduce(f32[]{:T(128)} %multiply_reduce_fusion), channel_id=1, replica_groups=mesh['fsdp'=8,'mat'=4] {'fsdp','mat'}, use_global_device_ids=true, to_apply=%region_2.0 | all-reduce | flops 1 | bytes 8 | tf_op jit(solution)/shard_map/psum | solution.py:28
  91.3 0.0 all-reduce.2.cloned.1.call-done
  91.3 0.0 copy-start.6
  91.3 277.5 %reduce-scatter.2.cloned.1.call-done = f32[2048,256]{0,1:T(8,128)} async-done(((f32[16384,256]{0,1:T(8,128)}), f32[2048,256]{0,1:T(8,128)}) %reduce-scatter.2.cloned.1.call-update) | async-done | bytes 2097168 | tf_op jit(solution)/shard_map/reduce_scatter | solution.py:37
  368.8 4.6 fusion.9
  373.5 0.0 copy-done
  373.5 0.0 copy-done.6
  373.5 0.0 copy-done.4
  373.5 0.0 copy-start.2
  373.5 4.1 divide_convert_fusion
  377.6 0.0 copy-done.2
  377.6 1.5 collective-permute-start
  379.1 23.3 %collective-permute-done = bf16[2048,256]{0,1:T(8,128)(2,1)} collective-permute-done((bf16[2048,256]{0,1:T(8,128)(2,1)S(1)}, bf16[2048,256]{0,1:T(8,128)(2,1)}, u32[]{:S(2)}, u32[]{:S(2)}) %collective-permute-start) | collective-permute-done | bytes 1048608 | tf_op jit(solution)/shard_map/ppermute | solution.py:14
  402.3 2.4 maximum_select_fusion.3
  404.7 0.9 collective-permute-start.1
  405.6 45.5 %collective-permute-done.1 = bf16[4096,256]{0,1:T(8,128)(2,1)} collective-permute-done((bf16[4096,256]{0,1:T(8,128)(2,1)S(1)}, bf16[4096,256]{0,1:T(8,128)(2,1)}, u32[]{:S(2)}, u32[]{:S(2)}) %collective-permute-start.1) | collective-permute-done | bytes 2097184 | tf_op jit(solution)/shard_map/ppermute | solution.py:14
  451.1 4.7 maximum_select_fusion.2
  455.8 2.2 collective-permute-start.2
  458.0 2.9 copy.10
  460.9 1.8 copy.11
  462.7 174.5 %collective-permute-done.2 = bf16[8192,256]{0,1:T(8,128)(2,1)} collective-permute-done((bf16[8192,256]{0,1:T(8,128)(2,1)}, bf16[8192,256]{0,1:T(8,128)(2,1)}, u32[]{:S(2)}, u32[]{:S(2)}) %collective-permute-start.2) | collective-permute-done | bytes 4194336 | tf_op jit(solution)/shard_map/ppermute | solution.py:14
  637.2 23.1 %convert_bitcast_fusion = bf16[1,1024,16384]{1,2,0:T(8,128)(2,1)} fusion(bf16[8192,256]{0,1:T(8,128)(2,1)} %collective-permute-done.2, bf16[8192,256]{0,1:T(8,128)(2,1)} %maximum_select_fusion.2, pred[]{:T(512)S(6)} %eq.9, bf16[1,1024,256]{2,1,0:T(8,128)(2,1)S(1)} %copy-done.5), kind=kOutput, calls=%fused_computation.3 | convolution fusion | flops 8644460544 | bytes 42467328 | tf_op jit(solution)/shard_map/dot_general | solution.py:48
  660.3 44.0 %copy.9 = bf16[1,1024,16384]{2,1,0:T(8,128)(2,1)} copy(bf16[1,1024,16384]{1,2,0:T(8,128)(2,1)} %convert_bitcast_fusion) | data formatting | bytes 67108864
  704.4 0.0 copy-done.1
  (6 shorter events, 0.0 us)
Async XLA Ops:
  7.2 366.3 %copy-start = (f32[1,2048,256]{2,1,0:T(8,128)S(1)}, f32[1,2048,256]{2,1,0:T(8,128)}, u32[]{:S(2)}) copy-start(f32[1,2048,256]{2,1,0:T(8,128)} %param.8) | copy-start | bytes 6291460
  7.2 84.1 %all-reduce.2.cloned.1.call-start = ((), (), s32[]{:S(2)}) async-start(), calls=%async_computation.1 | async-start | bytes 524288 | tf_op jit(solution)/shard_map/psum | solution.py:34
  9.6 359.2 %reduce-scatter.2.cloned.1.call-start = ((), (), s32[]{:S(2)}) async-start(), calls=%async_computation.2 | async-start | bytes 18874368 | tf_op jit(solution)/shard_map/reduce_scatter | solution.py:37
  91.3 282.2 %copy-start.6 = (f32[256,256]{1,0:T(8,128)S(1)}, f32[256,256]{1,0:T(8,128)}, u32[]{:S(2)}) copy-start(f32[256,256]{1,0:T(8,128)} %all-reduce.2.cloned.1.call-done) | copy-start | bytes 786436
  368.8 4.7 copy-start.4
  373.5 4.2 copy-start.2
  377.6 24.7 %collective-permute-start = (bf16[2048,256]{0,1:T(8,128)(2,1)S(1)}, bf16[2048,256]{0,1:T(8,128)(2,1)}, u32[]{:S(2)}, u32[]{:S(2)}) collective-permute-start(bf16[2048,256]{0,1:T(8,128)(2,1)S(1)} %get-tuple-element.6), channel_id=1, source_target_pairs={{0,4},{4,0},{8,12},{12,8},{16,20},{20,16},{24,28},{28,24},{1,5},{5... | collective-permute-start | bytes 3145736 | tf_op jit(solution)/shard_map/ppermute | solution.py:14
  404.7 46.4 %collective-permute-start.1 = (bf16[4096,256]{0,1:T(8,128)(2,1)S(1)}, bf16[4096,256]{0,1:T(8,128)(2,1)}, u32[]{:S(2)}, u32[]{:S(2)}) collective-permute-start(bf16[4096,256]{0,1:T(8,128)(2,1)S(1)} %maximum_select_fusion.3), channel_id=1, source_target_pairs={{0,8},{4,12},{8,0},{12,4},{16,24},{20,28},{24,16},{28,20},{1,9},{5... | collective-permute-start | bytes 6291464 | tf_op jit(solution)/shard_map/ppermute | solution.py:14
  455.8 5.1 copy-start.3
  455.8 181.4 %collective-permute-start.2 = (bf16[8192,256]{0,1:T(8,128)(2,1)}, bf16[8192,256]{0,1:T(8,128)(2,1)}, u32[]{:S(2)}, u32[]{:S(2)}) collective-permute-start(bf16[8192,256]{0,1:T(8,128)(2,1)} %maximum_select_fusion.2), channel_id=1, source_target_pairs={{0,16},{4,20},{8,24},{12,28},{16,0},{20,4},{24,8},{28,12},{1,17},{... | collective-permute-start | bytes 12582920 | tf_op jit(solution)/shard_map/ppermute | solution.py:14
  458.0 179.2 %copy-start.5 = (bf16[1,1024,256]{2,1,0:T(8,128)(2,1)S(1)}, bf16[1,1024,256]{2,1,0:T(8,128)(2,1)}, u32[]{:S(2)}) copy-start(bf16[1,1024,256]{2,1,0:T(8,128)(2,1)} %param.7) | copy-start | bytes 1572868
  660.3 44.1 %copy-start.1 = (f32[1,2048,256]{2,1,0:T(8,128)S(1)}, f32[1,2048,256]{2,1,0:T(8,128)}, u32[]{:S(2)}) copy-start(f32[1,2048,256]{2,1,0:T(8,128)} %param.8) | copy-start | bytes 6291460
Sparse Core Ops, SparseCore 0:
  11.9 73.7 all-reduce.1
  90.1 278.7 reduce-scatter.1
